TPU v7x, 256 devices: a whole 4x4x8 slice. The times are simulated.
256 devices in a mesh: section: 2 (over z_hi), dp: 16 (over z_lo, y), tensor: 8 (over x, core).
Axes of the slice: x: 4, y: 4, z: 8 (z_hi: 2, z_lo: 4; z = z_hi * 4 + z_lo), core: 2. Of those that a mesh axis runs over, the one named last changes fastest.
Arguments:
- section_input: bfloat16 [2, 1024, 8192], P('section', 'tensor', 'dp'), may hold values from -40 to 40
- norm_gain_attn: bfloat16 [2, 8192], P('section', 'dp'), may hold values from 0.099609375 to 1.8984375
- w_query: bfloat16 [2, 8192, 4096], P('section', 'dp', 'tensor'), may hold values from -0.0625 to 0.0625
- key_value_weight: bfloat16 [2, 2, 8192, 512], P('section', None, 'dp'), may hold values from -0.0625 to 0.0625
- w_output: bfloat16 [2, 4096, 8192], P('section', 'tensor', 'dp'), may hold values from -0.09375 to 0.09375
- norm_gain_ffn: bfloat16 [2, 8192], P('section', 'dp'), may hold values from 0.099609375 to 1.8984375
- w_gate_up: bfloat16 [2, 2, 8192, 14336], P('section', None, 'dp', 'tensor'), may hold values from -0.0625 to 0.0625
- w_down: bfloat16 [2, 14336, 8192], P('section', 'tensor', 'dp'), may hold values from -0.046875 to 0.046875
Outputs:
- section_output: bfloat16 [2, 1024, 8192], P('section', 'tensor', 'dp')
All inputs are finite; a program needn't handle non-finite values.
Results may differ from a plain program's by a relative error of at most 0.019.
Values may be sent and summed in bfloat16 or wider, within the bound.
A program may use at most 64 MiB of HBM per device.

v0:
```python
import math
import jax
import jax.numpy as jnp
from jax import lax
from jax.sharding import PartitionSpec as P

HEAD_SIZE = 128
QUERY_HEADS = 32
KEY_VALUE_HEADS = 4
EPS = 1e-05
THETA = 500000.0


def from_behind(x, axis, by):
    count = lax.axis_size(axis)
    return lax.ppermute(x, axis, [(i, (i + by) % count) for i in range(count)])


def apply_rotary(value_states, token_positions):
    width = value_states.shape[-1]
    half = width // 2
    freqs = jnp.exp(-(2.0 * jnp.arange(half, dtype=jnp.float32) / width) * math.log(THETA))
    angles = token_positions.astype(jnp.float32)[:, None] * freqs[None, :]
    cosine = jnp.cos(angles)[:, None, :]
    sine = jnp.sin(angles)[:, None, :]
    first = value_states[..., :half]
    second = value_states[..., half:]
    return jnp.concatenate(
        [first * cosine - second * sine, second * cosine + first * sine], axis=-1
    )


def local(
    section_input,
    norm_gain_attn,
    w_query,
    key_value_weight,
    w_output,
    norm_gain_ffn,
    w_gate_up,
    w_down,
):
    tile = section_input[0]
    rows_dev = tile.shape[0]
    cols_dev = tile.shape[1]
    tensor_count = lax.axis_size("tensor")
    data_count = lax.axis_size("dp")
    seq_total = rows_dev * tensor_count
    query_rows = seq_total // data_count
    width_total = cols_dev * data_count
    head_dim = HEAD_SIZE
    heads_dev = w_query.shape[2] // head_dim
    group_heads = QUERY_HEADS // KEY_VALUE_HEADS
    kv_dev = max(1, heads_dev // group_heads)
    per_kv = heads_dev // kv_dev
    tensor_pos = lax.axis_index("tensor")
    data_pos = lax.axis_index("dp")
    kv_first = tensor_pos * heads_dev // group_heads
    key_cols = lax.dynamic_slice_in_dim(
        key_value_weight[0], kv_first * head_dim, kv_dev * head_dim, 2
    )
    w_columns = jnp.concatenate([w_query[0], key_cols[0], key_cols[1]], axis=1)
    gain_attn = norm_gain_attn[0].astype(jnp.float32)[None, :]
    gain_ffn = norm_gain_ffn[0].astype(jnp.float32)[None, :]
    query_cols = heads_dev * head_dim
    kv_cols = kv_dev * head_dim
    query_pos = data_pos * query_rows + jnp.arange(query_rows, dtype=jnp.int32)
    all_pos = jnp.arange(seq_total, dtype=jnp.int32)
    arrived = from_behind(tile, "section", 1)
    wide = arrived.astype(jnp.float32)
    squares = lax.psum(jnp.sum(wide * wide, axis=1), "dp")
    normed_input = (wide * lax.rsqrt(squares / width_total + EPS)[:, None] * gain_attn).astype(
        jnp.bfloat16
    )
    partial_qkv = jnp.dot(
        lax.all_gather(normed_input, "tensor", axis=0, tiled=True),
        w_columns,
        preferred_element_type=jnp.float32,
    )
    query_sum = lax.psum_scatter(
        partial_qkv[:, :query_cols].astype(jnp.bfloat16), "dp", scatter_dimension=0, tiled=True
    ).astype(jnp.float32)
    key_sum = lax.psum(partial_qkv[:, query_cols:].astype(jnp.bfloat16), "dp").astype(jnp.float32)
    keys = apply_rotary(key_sum[:, :kv_cols].reshape(seq_total, kv_dev, head_dim), all_pos).astype(
        jnp.bfloat16
    )
    value_states = key_sum[:, kv_cols:].reshape(seq_total, kv_dev, head_dim).astype(jnp.bfloat16)
    query_states = apply_rotary(
        query_sum.reshape(query_rows, heads_dev, head_dim), query_pos
    ).astype(jnp.bfloat16)
    grouped = query_states.reshape(query_rows, kv_dev, per_kv, head_dim)
    scores = jnp.einsum(
        "qkgd,skd->kgqs", grouped, keys, preferred_element_type=jnp.float32
    ) * head_dim ** (-0.5)
    visible = all_pos[None, :] <= query_pos[:, None]
    weights_exp = jnp.where(visible, jnp.exp(scores), 0.0)
    probs = (weights_exp / jnp.sum(weights_exp, axis=-1, keepdims=True)).astype(jnp.bfloat16)
    mixed = (
        jnp.einsum("kgqs,skd->qkgd", probs, value_states, preferred_element_type=jnp.float32)
        .astype(jnp.bfloat16)
        .reshape(query_rows, query_cols)
    )
    attn_partial = jnp.dot(
        lax.all_gather(mixed, "dp", axis=0, tiled=True),
        w_output[0],
        preferred_element_type=jnp.float32,
    )
    attn = lax.psum_scatter(
        attn_partial.astype(jnp.bfloat16), "tensor", scatter_dimension=0, tiled=True
    ).astype(jnp.float32)
    resid = (arrived.astype(jnp.float32) + attn).astype(jnp.bfloat16)
    resid_wide = resid.astype(jnp.float32)
    squares_ffn = lax.psum(jnp.sum(resid_wide * resid_wide, axis=1), "dp")
    normed_ffn = (
        resid_wide * lax.rsqrt(squares_ffn / width_total + EPS)[:, None] * gain_ffn
    ).astype(jnp.bfloat16)
    rows_ffn = lax.all_gather(normed_ffn, "tensor", axis=0, tiled=True)
    ff_dev = w_gate_up.shape[3]
    summed = lax.psum_scatter(
        jnp.einsum("rd,gdf->rgf", rows_ffn, w_gate_up[0], preferred_element_type=jnp.float32)
        .reshape(query_rows * lax.axis_size("dp"), 2 * ff_dev)
        .astype(jnp.bfloat16),
        "dp",
        scatter_dimension=0,
        tiled=True,
    ).astype(jnp.float32)
    hidden = (jax.nn.silu(summed[:, :ff_dev]) * summed[:, ff_dev:]).astype(jnp.bfloat16)
    ffn_partial = jnp.dot(
        lax.all_gather(hidden, "dp", axis=0, tiled=True),
        w_down[0],
        preferred_element_type=jnp.float32,
    )
    ffn = lax.psum_scatter(
        ffn_partial.astype(jnp.bfloat16), "tensor", scatter_dimension=0, tiled=True
    ).astype(jnp.float32)
    result = (resid_wide + ffn).astype(jnp.bfloat16)
    return result[None]


def solution(mesh):
    placed = (
        P("section", "tensor", "dp"),
        P("section", "dp"),
        P("section", "dp", "tensor"),
        P("section", None, "dp", None),
        P("section", "tensor", "dp"),
        P("section", "dp"),
        P("section", None, "dp", "tensor"),
        P("section", "tensor", "dp"),
    )
    return jax.shard_map(
        local, mesh=mesh, in_specs=placed, out_specs=P("section", "tensor", "dp"), check_vma=False
    )
```

profile of v0, /device:TPU:8, one launch (start us, length us, event | category | flops | bytes accessed | tf_op | source)
XLA Modules:
  0.0 766.1 jit_solution(4502816704359785971)
XLA Ops:
  6.5 7.2 collective-permute-start
  13.7 0.7 mul.231
  14.4 3.1 collective-permute-done
  17.6 38.6 %psum.21 = f32[128]{0:T(128)S(1)} all-reduce(f32[128]{0:T(128)S(1)} %fusion.25), channel_id=1, replica_groups=mesh['section'=2,'dp'=16,'tensor'=8] {'dp'}, use_global_device_ids=true, to_apply=%region_1.2 | all-reduce | flops 128 | bytes 1024 | tf_op jit(solution)/shard_map/psum | solution.py:71
  56.2 0.8 fusion.27
  57.1 1.7 dynamic-slice_bitcast_fusion.1
  58.8 27.4 %all-gather.5.cloned.1.call-done = bf16[1024,512]{1,0:T(8,128)(2,1)} async-done(((bf16[128,512]{1,0:T(8,128)(2,1)}), bf16[1024,512]{1,0:T(8,128)(2,1)}) %all-gather.5.cloned.1.call-update) | async-done | bytes 1048592 | tf_op jit(solution)/shard_map/all_gather | solution.py:76
  86.2 2.4 convolution_convert_fusion.1
  88.7 0.8 slice.54
  89.6 1.0 slice.59
  91.1 160.4 %all-reduce.2.cloned.1.call-done = bf16[1024,256]{1,0:T(8,128)(2,1)} async-done(((bf16[1024,256]{1,0:T(8,128)(2,1)}), bf16[1024,256]{1,0:T(8,128)(2,1)}) %all-reduce.2.cloned.1.call-update) | async-done | bytes 524304 | tf_op jit(solution)/shard_map/psum | solution.py:83
  251.5 1.1 fusion.33
  252.6 2.4 fusion.37
  255.0 79.3 %reduce-scatter.5.cloned.1.call-done = bf16[64,512]{1,0:T(8,128)(2,1)} async-done(((bf16[1024,512]{1,0:T(8,128)(2,1)}), bf16[64,512]{1,0:T(8,128)(2,1)}) %reduce-scatter.5.cloned.1.call-update) | async-done | bytes 65552 | tf_op jit(solution)/shard_map/reduce_scatter | solution.py:80
  334.3 0.9 reshape.220
  336.4 0.6 copy.23
  337.1 81.5 %all-gather.7.cloned.1.call-done = bf16[1024,512]{1,0:T(8,128)(2,1)} async-done(((bf16[64,512]{1,0:T(8,128)(2,1)}), bf16[1024,512]{1,0:T(8,128)(2,1)}) %all-gather.7.cloned.1.call-update) | async-done | bytes 1048592 | tf_op jit(solution)/shard_map/all_gather | solution.py:104
  418.6 3.0 convolution_convert_fusion.2
  421.8 33.3 %reduce-scatter.7.cloned.1.call-done = bf16[128,512]{1,0:T(8,128)(2,1)} async-done(((bf16[1024,512]{1,0:T(8,128)(2,1)}), bf16[128,512]{1,0:T(8,128)(2,1)}) %reduce-scatter.7.cloned.1.call-update) | async-done | bytes 131088 | tf_op jit(solution)/shard_map/reduce_scatter | solution.py:108
  455.1 1.0 fusion.29
  456.1 39.0 %psum.23 = f32[128]{0:T(128)S(1)} all-reduce(f32[128]{0:T(128)S(1)} %fusion.29), channel_id=1, replica_groups=mesh['section'=2,'dp'=16,'tensor'=8] {'dp'}, use_global_device_ids=true, to_apply=%region_7.8 | all-reduce | flops 128 | bytes 1024 | tf_op jit(solution)/shard_map/psum | solution.py:113
  495.1 1.7 fusion.31
  496.8 6.0 copy.14
  502.8 18.1 %all-gather.9.cloned.1.call-done = bf16[1024,512]{1,0:T(8,128)(2,1)} async-done(((bf16[128,512]{1,0:T(8,128)(2,1)}), bf16[1024,512]{1,0:T(8,128)(2,1)}) %all-gather.9.cloned.1.call-update) | async-done | bytes 1048592 | tf_op jit(solution)/shard_map/all_gather | solution.py:117
  520.9 9.3 %convolution_convert_fusion = bf16[1024,3584]{1,0:T(8,128)(2,1)} fusion(bf16[1024,512]{1,0:T(8,128)(2,1)} %all-gather.9.cloned.1.call-done, bf16[3584,512]{1,0:T(8,128)(2,1)} %bitcast.64), kind=kOutput, calls=%fused_computation | convolution fusion | flops 3761766400 | bytes 12058624 | tf_op jit(solution)/shard_map/rd,gdf->rgf/dot_general | solution.py:120
  530.3 101.4 %reduce-scatter.9.cloned.1.call-done = bf16[64,3584]{1,0:T(8,128)(2,1)} async-done(((bf16[1024,3584]{1,0:T(8,128)(2,1)}), bf16[64,3584]{1,0:T(8,128)(2,1)}) %reduce-scatter.9.cloned.1.call-update) | async-done | bytes 458768 | tf_op jit(solution)/shard_map/reduce_scatter | solution.py:119
  631.7 1.1 convert_element_type.103
  632.8 0.8 fusion.24
  633.7 85.8 %all-gather.11.cloned.1.call-done = bf16[1024,1792]{1,0:T(8,128)(2,1)} async-done(((bf16[64,1792]{1,0:T(8,128)(2,1)}), bf16[1024,1792]{1,0:T(8,128)(2,1)}) %all-gather.11.cloned.1.call-update) | async-done | bytes 3670032 | tf_op jit(solution)/shard_map/all_gather | solution.py:129
  719.4 5.1 fusion.2
  724.5 33.5 %reduce-scatter.11.cloned.1.call-done = bf16[128,512]{1,0:T(8,128)(2,1)} async-done(((bf16[1024,512]{1,0:T(8,128)(2,1)}), bf16[128,512]{1,0:T(8,128)(2,1)}) %reduce-scatter.11.cloned.1.call-update) | async-done | bytes 131088 | tf_op jit(solution)/shard_map/reduce_scatter | solution.py:133
  758.0 1.6 fusion.38
  (41 shorter events, 2.1 us)
Async XLA Ops:
  6.5 712.9 %copy-start = (bf16[1,1792,512]{2,1,0:T(8,128)(2,1)S(1)}, bf16[1,1792,512]{2,1,0:T(8,128)(2,1)}, u32[]{:S(2)}) copy-start(bf16[1,1792,512]{2,1,0:T(8,128)(2,1)} %param.15) | copy-start | bytes 5505028
  6.5 79.7 %all-gather.5.cloned.1.call-start = ((), (), s32[]{:S(2)}) async-start(), calls=%async_computation.4 | async-start | bytes 1179648 | tf_op jit(solution)/shard_map/all_gather | solution.py:76
  6.5 11.0 %collective-permute-start = (bf16[128,512]{1,0:T(8,128)(2,1)}, bf16[128,512]{1,0:T(8,128)(2,1)S(1)}, u32[]{:S(2)}, u32[]{:S(2)}) collective-permute-start(bf16[128,512]{1,0:T(8,128)(2,1)} %bitcast.70), channel_id=1, source_target_pairs={{0,128},{128,0},{1,129},{129,1},{2,130},{130,2},{3,131},{131,3},{4... | collective-permute-start | bytes 393224 | tf_op jit(solution)/shard_map/ppermute | solution.py:16
  57.0 194.5 %all-reduce.2.cloned.1.call-start = ((), (), s32[]{:S(2)}) async-start(), calls=%async_computation.5 | async-start | bytes 1048576 | tf_op jit(solution)/shard_map/psum | solution.py:83
  89.5 244.8 %reduce-scatter.5.cloned.1.call-start = ((), (), s32[]{:S(2)}) async-start(), calls=%async_computation.6 | async-start | bytes 1114112 | tf_op jit(solution)/shard_map/reduce_scatter | solution.py:80
  90.7 328.0 %all-gather.7.cloned.1.call-start = ((), (), s32[]{:S(2)}) async-start(), calls=%async_computation.7 | async-start | bytes 1114112 | tf_op jit(solution)/shard_map/all_gather | solution.py:104
  251.5 84.5 %copy-start.2 = (bf16[1024,256]{1,0:T(8,128)(2,1)S(1)}, bf16[1024,256]{1,0:T(8,128)(2,1)}, u32[]{:S(2)}) copy-start(bf16[1024,256]{1,0:T(8,128)(2,1)} %all-reduce.2.cloned.1.call-done) | copy-start | bytes 1572868
  336.3 85.4 %copy-start.3 = (bf16[1,512]{1,0:T(2,128)(2,1)S(1)}, bf16[1,512]{1,0:T(2,128)(2,1)}, u32[]{:S(2)}) copy-start(bf16[1,512]{1,0:T(2,128)(2,1)} %param.13) | copy-start | bytes 3076
  337.1 118.0 %reduce-scatter.7.cloned.1.call-start = ((), (), s32[]{:S(2)}) async-start(), calls=%async_computation.8 | async-start | bytes 1179648 | tf_op jit(solution)/shard_map/reduce_scatter | solution.py:108
  421.7 99.2 %all-gather.9.cloned.1.call-start = ((), (), s32[]{:S(2)}) async-start(), calls=%async_computation.9 | async-start | bytes 1179648 | tf_op jit(solution)/shard_map/all_gather | solution.py:117
  496.7 134.9 %reduce-scatter.9.cloned.1.call-start = ((), (), s32[]{:S(2)}) async-start(), calls=%async_computation.10 | async-start | bytes 7798784 | tf_op jit(solution)/shard_map/reduce_scatter | solution.py:119
  530.3 189.1 %all-gather.11.cloned.1.call-start = ((), (), s32[]{:S(2)}) async-start(), calls=%async_computation.11 | async-start | bytes 3899392 | tf_op jit(solution)/shard_map/all_gather | solution.py:129
  633.6 124.4 %copy-start.1 = (bf16[128,512]{1,0:T(8,128)(2,1)S(1)}, bf16[128,512]{1,0:T(8,128)(2,1)}, u32[]{:S(2)}) copy-start(bf16[128,512]{1,0:T(8,128)(2,1)} %reduce-scatter.7.cloned.1.call-done) | copy-start | bytes 393220
  633.6 124.4 %reduce-scatter.11.cloned.1.call-start = ((), (), s32[]{:S(2)}) async-start(), calls=%async_computation.12 | async-start | bytes 1179648 | tf_op jit(solution)/shard_map/reduce_scatter | solution.py:133
Sparse Core Ops, SparseCore 0:
  57.2 29.0 all-gather.4
  89.7 161.8 all-reduce.1
  254.0 80.2 reduce-scatter.4
  337.2 81.3 all-gather.6
  421.8 33.1 reduce-scatter.6
  496.9 24.0 all-gather.8
  530.4 101.2 reduce-scatter.8
  633.7 85.6 all-gather.10
  724.7 33.2 reduce-scatter.10
where the time goes:
time: 767 us; the launch traced here: 766 us
  waiting for transfers between devices  624 us (81%)
  blocking collectives  77.6 us (10%)
  matrix products  20.8 us (3%)
  between operations  13.4 us (2%)
  other arithmetic  11.6 us (2%)
  local copies, waits for them, and re-layouts  11.3 us (1%)
    psum x1, waiting for transfers between devices, local(): lax.psum(partial_qkv[:, query_cols:].astype(jnp.bfloat16), 'dp')  160 us
    reduce_scatter x1, waiting for transfers between devices, local(): lax.psum_scatter(jnp.einsum('rd,gdf->rgf', rows_ffn, w_gate_up[0], prefer...  101 us
    all_gather x1, waiting for transfers between devices, local(): lax.all_gather(hidden, 'dp', axis=0, tiled=True)  85.8 us
    all_gather x1, waiting for transfers between devices, local(): lax.all_gather(mixed, 'dp', axis=0, tiled=True)  81.5 us
    reduce_scatter x1, waiting for transfers between devices, local(): lax.psum_scatter(partial_qkv[:, :query_cols].astype(jnp.bfloat16), 'dp',...  79.3 us
    psum x1, blocking collectives, local(): squares_ffn = lax.psum(jnp.sum(resid_wide * resid_wide, axis=1), 'dp')  39 us
    psum x1, blocking collectives, local(): squares = lax.psum(jnp.sum(wide * wide, axis=1), 'dp')  38.6 us
    reduce_scatter x1, waiting for transfers between devices, local(): lax.psum_scatter(ffn_partial.astype(jnp.bfloat16), 'tensor', scatter_dime...  33.5 us
  transfers between devices with their start and end apart: 10, of which 10 were waited for; matrix products, arithmetic and copies ran while one was open for 2% of the time, Pallas kernels for 0%

commit v1 on v0

--- a/solution.py
+++ b/solution.py
@@ -80,7 +80,9 @@
     query_sum = lax.psum_scatter(
         partial_qkv[:, :query_cols].astype(jnp.bfloat16), "dp", scatter_dimension=0, tiled=True
     ).astype(jnp.float32)
-    key_sum = lax.psum(partial_qkv[:, query_cols:].astype(jnp.bfloat16), "dp").astype(jnp.float32)
+    key_sum = jnp.sum(
+        lax.all_gather(partial_qkv[:, query_cols:].astype(jnp.bfloat16), "dp"), axis=0
+    ).astype(jnp.float32)
     keys = apply_rotary(key_sum[:, :kv_cols].reshape(seq_total, kv_dev, head_dim), all_pos).astype(
         jnp.bfloat16
     )

time: 767 us -> 711 us (0.927)
  waiting for transfers between devices: 624 us -> 564 us
    psum x1 -> x0, waiting for transfers between devices: 160 us -> none  [local(): lax.psum(partial_qkv[:, query_cols:].astype(jnp.bfloat16), 'dp')]
    all_gather x0 -> x1, waiting for transfers between devices: none -> 102 us  [local(): lax.all_gather(partial_qkv[:, query_cols:].astype(jnp.bfloat16), 'dp')]
  transfers between devices with their start and end apart: 10 -> 10, of which waited for: 10 -> 10; matrix products, arithmetic and copies ran while one was open for 2% -> 1% of each run, Pallas kernels for 0% -> 0%
where the time goes in v1:
time: 711 us; the launch traced here: 710 us
  waiting for transfers between devices  564 us (79%)
  blocking collectives  77.6 us (11%)
  matrix products  20.7 us (3%)
  other arithmetic  15.4 us (2%)
  between operations  13.4 us (2%)
  local copies, waits for them, and re-layouts  11.4 us (2%)
  starting transfers between devices  7.53 us (1%)
    all_gather x1, waiting for transfers between devices, local(): lax.all_gather(partial_qkv[:, query_cols:].astype(jnp.bfloat16), 'dp')  102 us
    reduce_scatter x1, waiting for transfers between devices, local(): lax.psum_scatter(jnp.einsum('rd,gdf->rgf', rows_ffn, w_gate_up[0], prefer...  101 us
    all_gather x1, waiting for transfers between devices, local(): lax.all_gather(hidden, 'dp', axis=0, tiled=True)  85.9 us
    reduce_scatter x1, waiting for transfers between devices, local(): lax.psum_scatter(partial_qkv[:, :query_cols].astype(jnp.bfloat16), 'dp',...  80.5 us
    all_gather x1, waiting for transfers between devices, local(): lax.all_gather(mixed, 'dp', axis=0, tiled=True)  79.7 us
    psum x1, blocking collectives, local(): squares_ffn = lax.psum(jnp.sum(resid_wide * resid_wide, axis=1), 'dp')  39 us
    psum x1, blocking collectives, local(): squares = lax.psum(jnp.sum(wide * wide, axis=1), 'dp')  38.6 us
    reduce_scatter x1, waiting for transfers between devices, local(): lax.psum_scatter(ffn_partial.astype(jnp.bfloat16), 'tensor', scatter_dime...  33.5 us
  transfers between devices with their start and end apart: 10, of which 10 were waited for; matrix products, arithmetic and copies ran while one was open for 1% of the time, Pallas kernels for 0%

profile of v1, /device:TPU:8, one launch (start us, length us, event | category | flops | bytes accessed | tf_op | source)
XLA Modules:
  0.0 710.2 jit_solution(13667671796648693740)
XLA Ops:
  6.5 7.2 %collective-permute-start = (bf16[128,512]{1,0:T(8,128)(2,1)}, bf16[128,512]{1,0:T(8,128)(2,1)S(1)}, u32[]{:S(2)}, u32[]{:S(2)}) collective-permute-start(bf16[128,512]{1,0:T(8,128)(2,1)} %bitcast.72), channel_id=1, source_target_pairs={{0,128},{128,0},{1,129},{129,1},{2,130},{130,2},{3,131},{131,3},{4... | collective-permute-start | bytes 393224 | tf_op jit(solution)/shard_map/ppermute | solution.py:16
  13.7 0.7 mul.231
  14.4 3.1 collective-permute-done
  17.6 38.6 %psum.14 = f32[128]{0:T(128)S(1)} all-reduce(f32[128]{0:T(128)S(1)} %fusion.25), channel_id=1, replica_groups=mesh['section'=2,'dp'=16,'tensor'=8] {'dp'}, use_global_device_ids=true, to_apply=%region_1.2 | all-reduce | flops 128 | bytes 1024 | tf_op jit(solution)/shard_map/psum | solution.py:71
  56.2 0.8 fusion.27
  57.1 1.7 dynamic-slice_bitcast_fusion.1
  58.8 27.4 %all-gather.7.cloned.1.call-done = bf16[1024,512]{1,0:T(8,128)(2,1)} async-done(((bf16[128,512]{1,0:T(8,128)(2,1)}), bf16[1024,512]{1,0:T(8,128)(2,1)}) %all-gather.7.cloned.1.call-update) | async-done | bytes 1048592 | tf_op jit(solution)/shard_map/all_gather | solution.py:76
  86.2 2.4 convolution_convert_fusion.1
  88.7 1.1 slice.59
  89.9 0.8 slice.54
  91.2 80.5 %reduce-scatter.5.cloned.1.call-done = bf16[64,512]{1,0:T(8,128)(2,1)} async-done(((bf16[1024,512]{1,0:T(8,128)(2,1)}), bf16[64,512]{1,0:T(8,128)(2,1)}) %reduce-scatter.5.cloned.1.call-update) | async-done | bytes 65552 | tf_op jit(solution)/shard_map/reduce_scatter | solution.py:80
  171.6 0.9 reshape.220
  172.7 101.7 %all-gather.15.cloned.1.call-done = bf16[16384,256]{1,0:T(8,128)(2,1)} async-done(((bf16[1024,256]{1,0:T(8,128)(2,1)}), bf16[16384,256]{1,0:T(8,128)(2,1)}) %all-gather.15.cloned.1.call-update) | async-done | bytes 8388624 | tf_op jit(solution)/shard_map/all_gather | solution.py:84
  274.4 4.8 reduce_sum.40
  279.3 2.4 fusion.37
  282.7 0.6 copy.23
  283.4 79.7 %all-gather.9.cloned.1.call-done = bf16[1024,512]{1,0:T(8,128)(2,1)} async-done(((bf16[64,512]{1,0:T(8,128)(2,1)}), bf16[1024,512]{1,0:T(8,128)(2,1)}) %all-gather.9.cloned.1.call-update) | async-done | bytes 1048592 | tf_op jit(solution)/shard_map/all_gather | solution.py:106
  363.1 2.9 convolution_convert_fusion.2
  366.1 33.3 %reduce-scatter.7.cloned.1.call-done = bf16[128,512]{1,0:T(8,128)(2,1)} async-done(((bf16[1024,512]{1,0:T(8,128)(2,1)}), bf16[128,512]{1,0:T(8,128)(2,1)}) %reduce-scatter.7.cloned.1.call-update) | async-done | bytes 131088 | tf_op jit(solution)/shard_map/reduce_scatter | solution.py:110
  399.4 1.0 fusion.29
  400.4 39.0 %psum.15 = f32[128]{0:T(128)S(1)} all-reduce(f32[128]{0:T(128)S(1)} %fusion.29), channel_id=1, replica_groups=mesh['section'=2,'dp'=16,'tensor'=8] {'dp'}, use_global_device_ids=true, to_apply=%region_7.8 | all-reduce | flops 128 | bytes 1024 | tf_op jit(solution)/shard_map/psum | solution.py:115
  439.4 1.7 fusion.31
  441.1 6.0 copy.14
  447.1 18.2 %all-gather.11.cloned.1.call-done = bf16[1024,512]{1,0:T(8,128)(2,1)} async-done(((bf16[128,512]{1,0:T(8,128)(2,1)}), bf16[1024,512]{1,0:T(8,128)(2,1)}) %all-gather.11.cloned.1.call-update) | async-done | bytes 1048592 | tf_op jit(solution)/shard_map/all_gather | solution.py:119
  465.3 9.3 %convolution_convert_fusion = bf16[1024,3584]{1,0:T(8,128)(2,1)} fusion(bf16[1024,512]{1,0:T(8,128)(2,1)} %all-gather.11.cloned.1.call-done, bf16[3584,512]{1,0:T(8,128)(2,1)} %bitcast.66), kind=kOutput, calls=%fused_computation | convolution fusion | flops 3761766400 | bytes 12058624 | tf_op jit(solution)/shard_map/rd,gdf->rgf/dot_general | solution.py:122
  474.7 100.9 %reduce-scatter.9.cloned.1.call-done = bf16[64,3584]{1,0:T(8,128)(2,1)} async-done(((bf16[1024,3584]{1,0:T(8,128)(2,1)}), bf16[64,3584]{1,0:T(8,128)(2,1)}) %reduce-scatter.9.cloned.1.call-update) | async-done | bytes 458768 | tf_op jit(solution)/shard_map/reduce_scatter | solution.py:121
  575.6 1.1 convert_element_type.105
  576.6 0.8 fusion.24
  577.5 85.9 %all-gather.13.cloned.1.call-done = bf16[1024,1792]{1,0:T(8,128)(2,1)} async-done(((bf16[64,1792]{1,0:T(8,128)(2,1)}), bf16[1024,1792]{1,0:T(8,128)(2,1)}) %all-gather.13.cloned.1.call-update) | async-done | bytes 3670032 | tf_op jit(solution)/shard_map/all_gather | solution.py:131
  663.5 5.1 fusion.2
  668.6 33.5 %reduce-scatter.11.cloned.1.call-done = bf16[128,512]{1,0:T(8,128)(2,1)} async-done(((bf16[1024,512]{1,0:T(8,128)(2,1)}), bf16[128,512]{1,0:T(8,128)(2,1)}) %reduce-scatter.11.cloned.1.call-update) | async-done | bytes 131088 | tf_op jit(solution)/shard_map/reduce_scatter | solution.py:135
  702.0 1.6 fusion.38
  (41 shorter events, 2.1 us)
Async XLA Ops:
  6.5 656.9 %copy-start = (bf16[1,1792,512]{2,1,0:T(8,128)(2,1)S(1)}, bf16[1,1792,512]{2,1,0:T(8,128)(2,1)}, u32[]{:S(2)}) copy-start(bf16[1,1792,512]{2,1,0:T(8,128)(2,1)} %param.15) | copy-start | bytes 5505028
  6.5 79.7 %all-gather.7.cloned.1.call-start = ((), (), s32[]{:S(2)}) async-start(), calls=%async_computation.4 | async-start | bytes 1179648 | tf_op jit(solution)/shard_map/all_gather | solution.py:76
  6.5 11.0 %collective-permute-start = (bf16[128,512]{1,0:T(8,128)(2,1)}, bf16[128,512]{1,0:T(8,128)(2,1)S(1)}, u32[]{:S(2)}, u32[]{:S(2)}) collective-permute-start(bf16[128,512]{1,0:T(8,128)(2,1)} %bitcast.72), channel_id=1, source_target_pairs={{0,128},{128,0},{1,129},{129,1},{2,130},{130,2},{3,131},{131,3},{4... | collective-permute-start | bytes 393224 | tf_op jit(solution)/shard_map/ppermute | solution.py:16
  57.0 114.6 %reduce-scatter.5.cloned.1.call-start = ((), (), s32[]{:S(2)}) async-start(), calls=%async_computation.5 | async-start | bytes 1114112 | tf_op jit(solution)/shard_map/reduce_scatter | solution.py:80
  89.8 184.6 %all-gather.15.cloned.1.call-start = ((), (), s32[]{:S(2)}) async-start(), calls=%async_computation.12 | async-start | bytes 8912896 | tf_op jit(solution)/shard_map/all_gather | solution.py:84
  90.7 272.4 %all-gather.9.cloned.1.call-start = ((), (), s32[]{:S(2)}) async-start(), calls=%async_computation.6 | async-start | bytes 1114112 | tf_op jit(solution)/shard_map/all_gather | solution.py:106
  281.7 81.4 %copy-start.3 = (bf16[1,512,512]{2,1,0:T(8,128)(2,1)S(1)}, bf16[1,512,512]{2,1,0:T(8,128)(2,1)}, u32[]{:S(2)}) copy-start(bf16[1,512,512]{2,1,0:T(8,128)(2,1)} %param.12) | copy-start | bytes 1572868
  282.6 83.5 %copy-start.2 = (bf16[1,512]{1,0:T(2,128)(2,1)S(1)}, bf16[1,512]{1,0:T(2,128)(2,1)}, u32[]{:S(2)}) copy-start(bf16[1,512]{1,0:T(2,128)(2,1)} %param.13) | copy-start | bytes 3076
  283.4 116.0 %reduce-scatter.7.cloned.1.call-start = ((), (), s32[]{:S(2)}) async-start(), calls=%async_computation.7 | async-start | bytes 1179648 | tf_op jit(solution)/shard_map/reduce_scatter | solution.py:110
  366.1 99.3 %all-gather.11.cloned.1.call-start = ((), (), s32[]{:S(2)}) async-start(), calls=%async_computation.8 | async-start | bytes 1179648 | tf_op jit(solution)/shard_map/all_gather | solution.py:119
  441.1 134.5 %reduce-scatter.9.cloned.1.call-start = ((), (), s32[]{:S(2)}) async-start(), calls=%async_computation.9 | async-start | bytes 7798784 | tf_op jit(solution)/shard_map/reduce_scatter | solution.py:121
  474.6 188.8 %all-gather.13.cloned.1.call-start = ((), (), s32[]{:S(2)}) async-start(), calls=%async_computation.10 | async-start | bytes 3899392 | tf_op jit(solution)/shard_map/all_gather | solution.py:131
  577.5 124.5 %copy-start.1 = (bf16[128,512]{1,0:T(8,128)(2,1)S(1)}, bf16[128,512]{1,0:T(8,128)(2,1)}, u32[]{:S(2)}) copy-start(bf16[128,512]{1,0:T(8,128)(2,1)} %reduce-scatter.7.cloned.1.call-done) | copy-start | bytes 393220
  577.5 124.5 %reduce-scatter.11.cloned.1.call-start = ((), (), s32[]{:S(2)}) async-start(), calls=%async_computation.11 | async-start | bytes 1179648 | tf_op jit(solution)/shard_map/reduce_scatter | solution.py:135
Sparse Core Ops, SparseCore 0:
  57.2 29.0 all-gather.6
  90.0 81.6 reduce-scatter.4
  173.4 100.9 all-gather.14
  283.5 79.5 all-gather.8
  366.2 33.1 reduce-scatter.6
  441.2 24.0 all-gather.10
  474.7 100.7 reduce-scatter.8
  577.6 85.8 all-gather.12
  668.7 33.2 reduce-scatter.10
